TPU v7x, 32 devices: a whole 2x2x4 slice. The times are simulated.
32 devices in a mesh: row: 8 (over z, y), col: 4 (over x, core).
Axes of the slice: x: 2, y: 2, z: 4, core: 2. Of those that a mesh axis runs over, the one named last changes fastest.
Arguments:
- momentum: float32 [8192, 8192], P('row', 'col'), may hold values from -6 to 6
- gradient: bfloat16 [8192, 8192], P('row', 'col'), may hold values from -6 to 6
- weight: bfloat16 [8192, 8192], P('row', 'col'), may hold values from -6 to 6
- right_start: float32 [8192, 512], P('col', 'row'), may hold values from -0.0625 to 0.0625
Outputs:
- new_momentum: float32 [8192, 8192], P('row', 'col')
- new_weight: bfloat16 [8192, 8192], P('row', 'col')
- new_right: float32 [8192, 512], P('col', 'row')
All inputs are finite; a program needn't handle non-finite values.
Results may differ from a plain program's by a relative error of at most 0.001.
Values sent between devices are 32-bit elements; how exact they have to be, the bound alone decides.
A program may use at most 128 MiB of HBM per device.

v0:
```python
import jax
import jax.numpy as jnp
from jax import lax
from jax.sharding import PartitionSpec as P

ITERS = 2
BLOCK = 128
gram_mode = lax.Precision.HIGHEST
wide_mode = lax.Precision.HIGH
momentum_decay = 0.9
step_rate = 0.1
epsilon = 1e-06


def self_gram(rows):
    return lax.dot_general(rows, rows, (((0,), (0,)), ((), ())), precision=gram_mode)


def times_transposed(a, b):
    return lax.dot_general(a, b, (((1,), (1,)), ((), ())), precision=gram_mode)


def solve_rows(rows, gram_sum):
    rank = gram_sum.shape[0]
    block = min(BLOCK, rank)
    trailing = gram_sum
    rest = rows
    solved = []
    for at in range(0, rank, block):
        size = min(block, rank - at)
        corner = lax.linalg.cholesky(trailing[:size, :size], symmetrize_input=False)
        inverse = lax.linalg.triangular_solve(
            corner, jnp.eye(size, dtype=corner.dtype), left_side=True, lower=True
        )
        block_rows = times_transposed(rest[:, :size], inverse)
        solved.append(block_rows)
        if at + size < rank:
            panel = times_transposed(trailing[size:, :size], inverse)
            trailing = trailing[size:, size:] - times_transposed(panel, panel)
            rest = rest[:, size:] - times_transposed(block_rows, panel)
    return jnp.concatenate(solved, axis=1)


def shards(momentum, gradient, weight, right_start):
    rows_at, cols_at = (lax.psum(1, "row"), lax.psum(1, "col"))
    out_dim, in_dim = (momentum.shape[0] * rows_at, momentum.shape[1] * cols_at)
    rank = right_start.shape[1] * rows_at
    blended = momentum + gradient.astype(jnp.float32)
    right_full = lax.all_gather(right_start, "row", axis=1, tiled=True)
    right_shard = right_start
    for iteration in range(ITERS):
        partials = jnp.dot(blended, right_full, precision=wide_mode)
        left_sum = lax.psum(partials, "col")
        gram_sum = lax.psum(self_gram(left_sum), "row")
        left_rows = solve_rows(left_sum, gram_sum)
        transposed = lax.dot_general(
            blended, left_rows, (((0,), (0,)), ((), ())), precision=wide_mode
        )
        products = lax.psum_scatter(transposed, "row", scatter_dimension=1, tiled=True)
        squares = lax.psum(jnp.sum(products * products, axis=0, keepdims=True), "col")
        col_norms = jnp.sqrt(squares + epsilon)
        right_shard = products / col_norms
        products_full, norms_full = (
            lax.all_gather(products, "row", axis=1, tiled=True),
            lax.all_gather(col_norms, "row", axis=1, tiled=True),
        )
        right_full = products_full / norms_full
    outer_dims = (((1,), (1,)), ((), ()))
    feedback = lax.dot_general(left_rows, products_full, outer_dims, precision=wide_mode)
    new_momentum = blended - (1.0 - momentum_decay) * feedback
    scale_factor = step_rate * (out_dim * in_dim / rank) ** 0.5
    update = lax.dot_general(left_rows, right_full, outer_dims, precision=wide_mode)
    new_weight = (weight.astype(jnp.float32) - scale_factor * update).astype(jnp.bfloat16)
    return (new_momentum, new_weight, right_shard)


def solution(mesh):
    return jax.shard_map(
        shards,
        mesh=mesh,
        in_specs=(P("row", "col"), P("row", "col"), P("row", "col"), P("col", "row")),
        out_specs=(P("row", "col"), P("row", "col"), P("col", "row")),
        check_vma=False,
    )
```

profile of v0, /device:TPU:0, one launch (start us, length us, event | category | flops | bytes accessed | tf_op | source)
XLA Modules:
  0.0 969.1 jit_solution(15669869728964990464)
XLA Ops:
  7.9 77.7 %all-gather.4.cloned.1.call-done = f32[2048,512]{0,1:T(8,128)} async-done(((f32[2048,64]{0,1:T(8,128)}), f32[2048,512]{0,1:T(8,128)}) %all-gather.4.cloned.1.call-update) | async-done | bytes 4194320 | tf_op jit(solution)/shard_map/all_gather | solution.py:49
  85.7 12.0 %fusion.75 = f32[1024,512]{1,0:T(8,128)} fusion(f32[2048,512]{0,1:T(8,128)} %all-gather.4.cloned.1.call-done, f32[1024,2048]{1,0:T(8,128)} %param.7, bf16[1024,2048]{1,0:T(8,128)(2,1)} %param.8), kind=kOutput, calls=%fused_computation.122 | convolution fusion | flops 6446645248 | bytes 18874368 | tf_op jit(solution)/shard_map/dot_general | solution.py:52
  97.7 50.0 %all-reduce.7.cloned.1.call-done = f32[1024,512]{1,0:T(8,128)} async-done(((f32[1024,512]{1,0:T(8,128)}), f32[1024,512]{1,0:T(8,128)}) %all-reduce.7.cloned.1.call-update) | async-done | bytes 2097168 | tf_op jit(solution)/shard_map/psum | solution.py:53
  154.7 78.3 %all-reduce.9.cloned.1.call-done = f32[512,512]{1,0:T(8,128)} async-done(((f32[512,512]{1,0:T(8,128)}), f32[512,512]{1,0:T(8,128)}) %all-reduce.9.cloned.1.call-update) | async-done | bytes 1048592 | tf_op jit(solution)/shard_map/psum | solution.py:54
  233.8 11.7 %custom-call.20 = f32[128,128]{1,0:T(8,128)S(1)} custom-call(f32[128,128]{1,0:T(8,128)S(1)} %slice.125), custom_call_target="Cholesky" | custom-call | tf_op jit(solution)/shard_map/cholesky/custom-call.1 | solution.py:31
  259.9 11.7 %custom-call.22 = f32[128,128]{1,0:T(8,128)S(1)} custom-call(f32[128,128]{1,0:T(8,128)S(1)} %slice.130), custom_call_target="Cholesky" | custom-call | tf_op jit(solution)/shard_map/cholesky/custom-call.1 | solution.py:31
  284.2 11.7 %custom-call.24 = f32[128,128]{1,0:T(8,128)S(1)} custom-call(f32[128,128]{1,0:T(8,128)S(1)} %slice.135), custom_call_target="Cholesky" | custom-call | tf_op jit(solution)/shard_map/cholesky/custom-call.1 | solution.py:31
  307.9 11.7 %custom-call.26 = f32[128,128]{1,0:T(8,128)S(1)} custom-call(f32[128,128]{1,0:T(8,128)S(1)} %convolution_subtract_fusion.9), custom_call_target="Cholesky" | custom-call | tf_op jit(solution)/shard_map/cholesky/custom-call.1 | solution.py:31
  337.7 11.1 %fusion.3 = f32[2048,512]{0,1:T(8,128)} fusion(f32[1024,128]{0,1:T(8,128)S(1)} %fusion.77, f32[1024,128]{0,1:T(8,128)S(1)} %fusion.19, f32[1024,128]{0,1:T(8,128)S(1)} %fusion.21, f32[1024,128]{0,1:T(8,128)S(1)} %fusion.23, f32[1024,2048]{1,0:T(8,128)} %param.7, bf16[1024,2048]{1,0:T(8,128)(2,1)S(1)} %copy-done), kind=kOutput, calls=%fused_computation.6 | convolution fusion | flops 6448218112 | bytes 18874368 | tf_op jit(solution)/shard_map/dot_general | solution.py:56
  348.8 88.0 %reduce-scatter.3.cloned.1.call-done = f32[2048,64]{0,1:T(8,128)} async-done(((f32[2048,512]{0,1:T(8,128)}), f32[2048,64]{0,1:T(8,128)}) %reduce-scatter.3.cloned.1.call-update) | async-done | bytes 524304 | tf_op jit(solution)/shard_map/reduce_scatter | solution.py:59
  445.6 21.6 %all-reduce = f32[512]{0:T(512)S(1)} all-reduce(f32[512]{0:T(512)S(1)} %bitcast_dynamic-update-slice_fusion), channel_id=1, replica_groups=mesh['row'=8,'col'=4] {'row'}, use_global_device_ids=true, to_apply=%add | all-reduce | flops 512 | bytes 4096
  467.2 44.4 %all-gather.6.cloned.1.call-done = f32[2048,512]{0,1:T(8,128)} async-done(((f32[2048,64]{0,1:T(8,128)}), f32[2048,512]{0,1:T(8,128)}) %all-gather.6.cloned.1.call-update) | async-done | bytes 4194320 | tf_op jit(solution)/shard_map/all_gather | solution.py:64
  511.6 12.2 %fusion.1 = f32[1024,512]{1,0:T(8,128)} fusion(f32[2048,512]{0,1:T(8,128)} %all-gather.6.cloned.1.call-done, f32[512]{0:T(512)S(1)} %all-reduce, f32[1024,2048]{1,0:T(8,128)} %param.7, bf16[1024,2048]{1,0:T(8,128)(2,1)} %param.8), kind=kOutput, calls=%fused_computation.4 | convolution fusion | flops 6447693824 | bytes 18876416 | tf_op jit(solution)/shard_map/dot_general | solution.py:52
  523.8 50.0 %all-reduce.11.cloned.1.call-done = f32[1024,512]{1,0:T(8,128)} async-done(((f32[1024,512]{1,0:T(8,128)}), f32[1024,512]{1,0:T(8,128)}) %all-reduce.11.cloned.1.call-update) | async-done | bytes 2097168 | tf_op jit(solution)/shard_map/psum | solution.py:53
  581.0 78.1 %all-reduce.13.cloned.1.call-done = f32[512,512]{1,0:T(8,128)} async-done(((f32[512,512]{1,0:T(8,128)}), f32[512,512]{1,0:T(8,128)}) %all-reduce.13.cloned.1.call-update) | async-done | bytes 1048592 | tf_op jit(solution)/shard_map/psum | solution.py:54
  659.9 11.7 %custom-call.28 = f32[128,128]{1,0:T(8,128)S(1)} custom-call(f32[128,128]{1,0:T(8,128)S(1)} %slice.140), custom_call_target="Cholesky" | custom-call | tf_op jit(solution)/shard_map/cholesky/custom-call.1 | solution.py:31
  686.1 11.7 %custom-call.30 = f32[128,128]{1,0:T(8,128)S(1)} custom-call(f32[128,128]{1,0:T(8,128)S(1)} %slice.145), custom_call_target="Cholesky" | custom-call | tf_op jit(solution)/shard_map/cholesky/custom-call.1 | solution.py:31
  710.7 11.7 %custom-call.32 = f32[128,128]{1,0:T(8,128)S(1)} custom-call(f32[128,128]{1,0:T(8,128)S(1)} %slice.150), custom_call_target="Cholesky" | custom-call | tf_op jit(solution)/shard_map/cholesky/custom-call.1 | solution.py:31
  734.4 11.7 %custom-call.34 = f32[128,128]{1,0:T(8,128)S(1)} custom-call(f32[128,128]{1,0:T(8,128)S(1)} %convolution_subtract_fusion.8), custom_call_target="Cholesky" | custom-call | tf_op jit(solution)/shard_map/cholesky/custom-call.1 | solution.py:31
  765.0 10.9 %fusion.25 = f32[2048,512]{0,1:T(8,128)} fusion(f32[1024,128]{0,1:T(8,128)S(1)} %fusion.79, f32[1024,128]{0,1:T(8,128)S(1)} %fusion.13, f32[1024,128]{0,1:T(8,128)S(1)} %fusion.15, f32[1024,128]{0,1:T(8,128)S(1)} %fusion.17, f32[1024,2048]{1,0:T(8,128)} %param.7, bf16[1024,2048]{1,0:T(8,128)(2,1)S(1)} %copy-done.1), kind=kOutput, calls=%fused_computation.43 | convolution fusion | flops 6448218112 | bytes 18874368 | tf_op jit(solution)/shard_map/dot_general | solution.py:56
  776.0 88.0 %reduce-scatter.5.cloned.1.call-done = f32[2048,64]{0,1:T(8,128)} async-done(((f32[2048,512]{0,1:T(8,128)}), f32[2048,64]{0,1:T(8,128)}) %reduce-scatter.5.cloned.1.call-update) | async-done | bytes 524304 | tf_op jit(solution)/shard_map/reduce_scatter | solution.py:59
  871.5 21.6 %all-reduce.1 = f32[512]{0:T(512)S(1)} all-reduce(f32[512]{0:T(512)S(1)} %fusion.74), channel_id=1, replica_groups=mesh['row'=8,'col'=4] {'row'}, use_global_device_ids=true, to_apply=%add.1 | all-reduce | flops 512 | bytes 4096
  895.0 43.9 %all-gather.8.cloned.1.call-done = f32[2048,512]{0,1:T(8,128)} async-done(((f32[2048,64]{0,1:T(8,128)}), f32[2048,512]{0,1:T(8,128)}) %all-gather.8.cloned.1.call-update) | async-done | bytes 4194320 | tf_op jit(solution)/shard_map/all_gather | solution.py:64
  938.9 13.9 %multiply_subtract_fusion = f32[1024,2048]{1,0:T(8,128)} fusion(f32[2048,512]{0,1:T(8,128)} %all-gather.8.cloned.1.call-done, f32[1024,128]{0,1:T(8,128)S(1)} %fusion.79, f32[1024,128]{0,1:T(8,128)S(1)} %fusion.13, f32[1024,128]{0,1:T(8,128)S(1)} %fusion.15, f32[1024,128]{0,1:T(8,128)S(1)} %fusion.17, f32[1024,2048]{1,0:T(8,128)} %param.7, ...), kind=kOutput, calls=%fused_computation.1 | convolution fusion | flops 6452412416 | bytes 27262976 | tf_op jit(solution)/shard_map/dot_general | solution.py:69
  (124 shorter events, 158.3 us)
Async XLA Ops:
  7.2 78.5 %all-gather.4.cloned.1.call-start = ((), (), s32[]{:S(2)}) async-start(), calls=%async_computation.2 | async-start | bytes 4718592 | tf_op jit(solution)/shard_map/all_gather | solution.py:49
  7.9 139.8 %all-reduce.7.cloned.1.call-start = ((), (), s32[]{:S(2)}) async-start(), calls=%async_computation.3 | async-start | bytes 4194304 | tf_op jit(solution)/shard_map/psum | solution.py:53
  97.7 135.3 %all-reduce.9.cloned.1.call-start = ((), (), s32[]{:S(2)}) async-start(), calls=%async_computation.4 | async-start | bytes 2097152 | tf_op jit(solution)/shard_map/psum | solution.py:54
  154.4 176.8 %copy-start.2 = (f32[1024,512]{1,0:T(8,128)S(1)}, f32[1024,512]{1,0:T(8,128)}, u32[]{:S(2)}) copy-start(f32[1024,512]{1,0:T(8,128)} %all-reduce.7.cloned.1.call-done) | copy-start | bytes 6291460
  154.4 282.4 %reduce-scatter.3.cloned.1.call-start = ((), (), s32[]{:S(2)}) async-start(), calls=%async_computation.5 | async-start | bytes 4718592 | tf_op jit(solution)/shard_map/reduce_scatter | solution.py:59
  333.7 3.9 copy-start
  348.7 88.2 %copy-start.9 = (u32[32]{0:T(128)S(1)}, u32[32]{0:T(128)}, u32[]{:S(2)}) copy-start(u32[32]{0:T(128)} %constant.27) | copy-start | bytes 388
  348.8 162.8 %all-gather.6.cloned.1.call-start = ((), (), s32[]{:S(2)}) async-start(), calls=%async_computation.6 | async-start | bytes 4718592 | tf_op jit(solution)/shard_map/all_gather | solution.py:64
  436.8 137.0 %all-reduce.11.cloned.1.call-start = ((), (), s32[]{:S(2)}) async-start(), calls=%async_computation.7 | async-start | bytes 4194304 | tf_op jit(solution)/shard_map/psum | solution.py:53
  523.8 135.3 %all-reduce.13.cloned.1.call-start = ((), (), s32[]{:S(2)}) async-start(), calls=%async_computation.8 | async-start | bytes 2097152 | tf_op jit(solution)/shard_map/psum | solution.py:54
  580.5 177.2 %copy-start.3 = (f32[1024,512]{1,0:T(8,128)S(1)}, f32[1024,512]{1,0:T(8,128)}, u32[]{:S(2)}) copy-start(f32[1024,512]{1,0:T(8,128)} %all-reduce.11.cloned.1.call-done) | copy-start | bytes 6291460
  580.5 283.5 %reduce-scatter.5.cloned.1.call-start = ((), (), s32[]{:S(2)}) async-start(), calls=%async_computation.9 | async-start | bytes 4718592 | tf_op jit(solution)/shard_map/reduce_scatter | solution.py:59
  683.0 26.3 %copy-start.5 = (f32[128,128]{1,0:T(8,128)}, f32[128,128]{1,0:T(8,128)S(1)}, u32[]{:S(2)}) copy-start(f32[128,128]{1,0:T(8,128)S(1)} %fusion.32) | copy-start | bytes 196612
  709.4 0.6 copy-start.6
  710.7 50.4 %copy-start.7 = (f32[128,128]{1,0:T(8,128)S(1)}, f32[128,128]{1,0:T(8,128)}, u32[]{:S(2)}) copy-start(f32[128,128]{1,0:T(8,128)} %copy-done.6) | copy-start | bytes 196612
  761.1 3.9 copy-start.1
  775.9 162.9 %all-gather.8.cloned.1.call-start = ((), (), s32[]{:S(2)}) async-start(), calls=%async_computation.10 | async-start | bytes 4718592 | tf_op jit(solution)/shard_map/all_gather | solution.py:64
  938.9 13.9 %copy-start.4 = (f32[2048,512]{0,1:T(8,128)S(1)}, f32[2048,512]{0,1:T(8,128)}, u32[]{:S(2)}) copy-start(f32[2048,512]{0,1:T(8,128)} %all-gather.8.cloned.1.call-done) | copy-start | bytes 12582916
  938.9 13.9 %copy-start.8 = (bf16[1024,2048]{1,0:T(8,128)(2,1)S(1)}, bf16[1024,2048]{1,0:T(8,128)(2,1)}, u32[]{:S(2)}) copy-start(bf16[1024,2048]{1,0:T(8,128)(2,1)} %param.9) | copy-start | bytes 12582916
Sparse Core Ops, SparseCore 0:
  10.1 75.5 all-gather.3
  97.8 49.9 all-reduce.6
  154.5 78.3 all-reduce.8
  348.9 87.8 reduce-scatter.2
  438.8 72.7 all-gather.5
  523.9 49.8 all-reduce.10
  580.6 78.3 all-reduce.12
  776.0 87.8 reduce-scatter.4
  866.1 72.6 all-gather.7
where the time goes:
time: 975 us; the launch traced here: 969 us
  waiting for transfers between devices  599 us (61%)
  other arithmetic  188 us (19%)
  matrix products  107 us (11%)
  blocking collectives  55.5 us (6%)
  between operations  15.6 us (2%)
    reduce_scatter x2, waiting for transfers between devices, shards(): lax.psum_scatter(transposed, 'row', scatter_dimension=1, tiled=True)  176 us
    psum x2, waiting for transfers between devices, shards(): gram_sum = lax.psum(self_gram(left_sum), 'row')  156 us
    psum x2, waiting for transfers between devices, shards(): left_sum = lax.psum(partials, 'col')  100 us
    another operation x24, other arithmetic, solve_rows(): corner = lax.linalg.cholesky(trailing[:size, :size], symmetrize_input=False)  99.1 us
    all_gather x2, waiting for transfers between devices, shards(): lax.all_gather(products, 'row', axis=1, tiled=True)  88.2 us
    another operation x16, other arithmetic, solve_rows(): lax.linalg.triangular_solve(corner, jnp.eye(size, dtype=corner.dtype), le...  84.4 us
    all_gather x1, waiting for transfers between devices, shards(): right_full = lax.all_gather(right_start, 'row', axis=1, tiled=True)  77.7 us
    unnamed x2, blocking collectives  43.1 us
  transfers between devices with their start and end apart: 9, of which 9 were waited for; matrix products, arithmetic and copies ran while one was open for 1% of the time, Pallas kernels for 0%

commit v1 on v0

--- a/solution.py
+++ b/solution.py
@@ -51,7 +51,7 @@
     for iteration in range(ITERS):
         partials = jnp.dot(blended, right_full, precision=wide_mode)
         left_sum = lax.psum(partials, "col")
-        gram_sum = lax.psum(self_gram(left_sum), "row")
+        gram_sum = jnp.sum(lax.all_gather(self_gram(left_sum), "row"), axis=0)
         left_rows = solve_rows(left_sum, gram_sum)
         transposed = lax.dot_general(
             blended, left_rows, (((0,), (0,)), ((), ())), precision=wide_mode

time: 975 us -> 1070 us (1.097)
  waiting for transfers between devices: 599 us -> 689 us
    all_gather x0 -> x2, waiting for transfers between devices: none -> 249 us  [shards(): gram_sum = jnp.sum(lax.all_gather(self_gram(left_sum), 'row'), axis=0)]
    psum x2 -> x0, waiting for transfers between devices: 156 us -> none  [shards(): gram_sum = lax.psum(self_gram(left_sum), 'row')]
  transfers between devices with their start and end apart: 9 -> 9, of which waited for: 9 -> 9; matrix products, arithmetic and copies ran while one was open for 1% -> 0% of each run, Pallas kernels for 0% -> 0%
where the time goes in v1:
time: 1070 us
  waiting for transfers between devices  689 us (64%)
  other arithmetic  197 us (18%)
  matrix products  106 us (10%)
  blocking collectives  55.5 us (5%)
  between operations  15.4 us (1%)
    all_gather x2, waiting for transfers between devices, shards(): gram_sum = jnp.sum(lax.all_gather(self_gram(left_sum), 'row'), axis=0)  249 us
    reduce_scatter x2, waiting for transfers between devices, shards(): lax.psum_scatter(transposed, 'row', scatter_dimension=1, tiled=True)  173 us
    psum x2, waiting for transfers between devices, shards(): left_sum = lax.psum(partials, 'col')  100 us
    another operation x24, other arithmetic, solve_rows(): corner = lax.linalg.cholesky(trailing[:size, :size], symmetrize_input=False)  99.5 us
    all_gather x2, waiting for transfers between devices, shards(): lax.all_gather(products, 'row', axis=1, tiled=True)  88.2 us
    another operation x16, other arithmetic, solve_rows(): lax.linalg.triangular_solve(corner, jnp.eye(size, dtype=corner.dtype), le...  84.3 us
    all_gather x1, waiting for transfers between devices, shards(): right_full = lax.all_gather(right_start, 'row', axis=1, tiled=True)  77.7 us
    unnamed x2, blocking collectives  43.2 us
  transfers between devices with their start and end apart: 9, of which 9 were waited for; matrix products, arithmetic and copies ran while one was open for 0% of the time, Pallas kernels for 0%

profile of v1, /device:TPU:0, one launch (start us, length us, event | category | flops | bytes accessed | tf_op | source)
XLA Modules:
  0.0 1066.0 jit_solution(6857507136681068155)
XLA Ops:
  7.9 77.7 %all-gather.8.cloned.1.call-done = f32[2048,512]{0,1:T(8,128)} async-done(((f32[2048,64]{0,1:T(8,128)}), f32[2048,512]{0,1:T(8,128)}) %all-gather.8.cloned.1.call-update) | async-done | bytes 4194320 | tf_op jit(solution)/shard_map/all_gather | solution.py:49
  85.7 12.0 %fusion.75 = f32[1024,512]{1,0:T(8,128)} fusion(f32[2048,512]{0,1:T(8,128)} %all-gather.8.cloned.1.call-done, f32[1024,2048]{1,0:T(8,128)} %param.7, bf16[1024,2048]{1,0:T(8,128)(2,1)} %param.8), kind=kOutput, calls=%fused_computation.122 | convolution fusion | flops 6446645248 | bytes 18874368 | tf_op jit(solution)/shard_map/dot_general | solution.py:52
  97.7 50.0 %all-reduce.5.cloned.1.call-done = f32[1024,512]{1,0:T(8,128)} async-done(((f32[1024,512]{1,0:T(8,128)}), f32[1024,512]{1,0:T(8,128)}) %all-reduce.5.cloned.1.call-update) | async-done | bytes 2097168 | tf_op jit(solution)/shard_map/psum | solution.py:53
  154.7 124.5 %all-gather.14.cloned.1.call-done = f32[4096,512]{1,0:T(8,128)} async-done(((f32[512,512]{1,0:T(8,128)}), f32[4096,512]{1,0:T(8,128)}) %all-gather.14.cloned.1.call-update) | async-done | bytes 8388624 | tf_op jit(solution)/shard_map/all_gather | solution.py:54
  283.7 11.7 %custom-call.20 = f32[128,128]{1,0:T(8,128)S(1)} custom-call(f32[128,128]{1,0:T(8,128)S(1)} %slice.125), custom_call_target="Cholesky" | custom-call | tf_op jit(solution)/shard_map/cholesky/custom-call.1 | solution.py:31
  308.7 11.7 %custom-call.22 = f32[128,128]{1,0:T(8,128)S(1)} custom-call(f32[128,128]{1,0:T(8,128)S(1)} %slice.130), custom_call_target="Cholesky" | custom-call | tf_op jit(solution)/shard_map/cholesky/custom-call.1 | solution.py:31
  334.8 11.7 %custom-call.24 = f32[128,128]{1,0:T(8,128)S(1)} custom-call(f32[128,128]{1,0:T(8,128)S(1)} %slice.135), custom_call_target="Cholesky" | custom-call | tf_op jit(solution)/shard_map/cholesky/custom-call.1 | solution.py:31
  358.5 11.9 %custom-call.26 = f32[128,128]{1,0:T(8,128)S(1)} custom-call(f32[128,128]{1,0:T(8,128)S(1)} %convolution_subtract_fusion.9), custom_call_target="Cholesky" | custom-call | tf_op jit(solution)/shard_map/cholesky/custom-call.1 | solution.py:31
  388.3 11.1 %fusion.3 = f32[2048,512]{0,1:T(8,128)} fusion(f32[1024,128]{0,1:T(8,128)S(1)} %fusion.77, f32[1024,128]{0,1:T(8,128)S(1)} %fusion.19, f32[1024,128]{0,1:T(8,128)S(1)} %fusion.21, f32[1024,128]{0,1:T(8,128)S(1)} %fusion.23, f32[1024,2048]{1,0:T(8,128)} %param.7, bf16[1024,2048]{1,0:T(8,128)(2,1)S(1)} %copy-done), kind=kOutput, calls=%fused_computation.6 | convolution fusion | flops 6448218112 | bytes 18874368 | tf_op jit(solution)/shard_map/dot_general | solution.py:56
  399.4 86.6 %reduce-scatter.3.cloned.1.call-done = f32[2048,64]{0,1:T(8,128)} async-done(((f32[2048,512]{0,1:T(8,128)}), f32[2048,64]{0,1:T(8,128)}) %reduce-scatter.3.cloned.1.call-update) | async-done | bytes 524304 | tf_op jit(solution)/shard_map/reduce_scatter | solution.py:59
  494.8 21.6 %all-reduce = f32[512]{0:T(512)S(1)} all-reduce(f32[512]{0:T(512)S(1)} %bitcast_dynamic-update-slice_fusion), channel_id=1, replica_groups=mesh['row'=8,'col'=4] {'row'}, use_global_device_ids=true, to_apply=%add | all-reduce | flops 512 | bytes 4096
  516.4 44.4 %all-gather.10.cloned.1.call-done = f32[2048,512]{0,1:T(8,128)} async-done(((f32[2048,64]{0,1:T(8,128)}), f32[2048,512]{0,1:T(8,128)}) %all-gather.10.cloned.1.call-update) | async-done | bytes 4194320 | tf_op jit(solution)/shard_map/all_gather | solution.py:64
  560.7 12.2 %fusion.1 = f32[1024,512]{1,0:T(8,128)} fusion(f32[2048,512]{0,1:T(8,128)} %all-gather.10.cloned.1.call-done, f32[512]{0:T(512)S(1)} %all-reduce, f32[1024,2048]{1,0:T(8,128)} %param.7, bf16[1024,2048]{1,0:T(8,128)(2,1)} %param.8), kind=kOutput, calls=%fused_computation.4 | convolution fusion | flops 6447693824 | bytes 18876416 | tf_op jit(solution)/shard_map/dot_general | solution.py:52
  573.0 50.0 %all-reduce.7.cloned.1.call-done = f32[1024,512]{1,0:T(8,128)} async-done(((f32[1024,512]{1,0:T(8,128)}), f32[1024,512]{1,0:T(8,128)}) %all-reduce.7.cloned.1.call-update) | async-done | bytes 2097168 | tf_op jit(solution)/shard_map/psum | solution.py:53
  630.2 124.3 %all-gather.16.cloned.1.call-done = f32[4096,512]{1,0:T(8,128)} async-done(((f32[512,512]{1,0:T(8,128)}), f32[4096,512]{1,0:T(8,128)}) %all-gather.16.cloned.1.call-update) | async-done | bytes 8388624 | tf_op jit(solution)/shard_map/all_gather | solution.py:54
  759.0 11.7 %custom-call.28 = f32[128,128]{1,0:T(8,128)S(1)} custom-call(f32[128,128]{1,0:T(8,128)S(1)} %slice.140), custom_call_target="Cholesky" | custom-call | tf_op jit(solution)/shard_map/cholesky/custom-call.1 | solution.py:31
  784.0 11.7 %custom-call.30 = f32[128,128]{1,0:T(8,128)S(1)} custom-call(f32[128,128]{1,0:T(8,128)S(1)} %slice.145), custom_call_target="Cholesky" | custom-call | tf_op jit(solution)/shard_map/cholesky/custom-call.1 | solution.py:31
  809.8 11.7 %custom-call.32 = f32[128,128]{1,0:T(8,128)S(1)} custom-call(f32[128,128]{1,0:T(8,128)S(1)} %slice.150), custom_call_target="Cholesky" | custom-call | tf_op jit(solution)/shard_map/cholesky/custom-call.1 | solution.py:31
  833.5 11.9 %custom-call.34 = f32[128,128]{1,0:T(8,128)S(1)} custom-call(f32[128,128]{1,0:T(8,128)S(1)} %convolution_subtract_fusion.8), custom_call_target="Cholesky" | custom-call | tf_op jit(solution)/shard_map/cholesky/custom-call.1 | solution.py:31
  863.3 10.9 %fusion.25 = f32[2048,512]{0,1:T(8,128)} fusion(f32[1024,128]{0,1:T(8,128)S(1)} %fusion.79, f32[1024,128]{0,1:T(8,128)S(1)} %fusion.13, f32[1024,128]{0,1:T(8,128)S(1)} %fusion.15, f32[1024,128]{0,1:T(8,128)S(1)} %fusion.17, f32[1024,2048]{1,0:T(8,128)} %param.7, bf16[1024,2048]{1,0:T(8,128)(2,1)S(1)} %copy-done.1), kind=kOutput, calls=%fused_computation.43 | convolution fusion | flops 6448218112 | bytes 18874368 | tf_op jit(solution)/shard_map/dot_general | solution.py:56
  874.3 86.6 %reduce-scatter.5.cloned.1.call-done = f32[2048,64]{0,1:T(8,128)} async-done(((f32[2048,512]{0,1:T(8,128)}), f32[2048,64]{0,1:T(8,128)}) %reduce-scatter.5.cloned.1.call-update) | async-done | bytes 524304 | tf_op jit(solution)/shard_map/reduce_scatter | solution.py:59
  968.4 21.6 %all-reduce.1 = f32[512]{0:T(512)S(1)} all-reduce(f32[512]{0:T(512)S(1)} %fusion.74), channel_id=1, replica_groups=mesh['row'=8,'col'=4] {'row'}, use_global_device_ids=true, to_apply=%add.1 | all-reduce | flops 512 | bytes 4096
  991.9 43.8 %all-gather.12.cloned.1.call-done = f32[2048,512]{0,1:T(8,128)} async-done(((f32[2048,64]{0,1:T(8,128)}), f32[2048,512]{0,1:T(8,128)}) %all-gather.12.cloned.1.call-update) | async-done | bytes 4194320 | tf_op jit(solution)/shard_map/all_gather | solution.py:64
  1035.8 13.9 %multiply_subtract_fusion = f32[1024,2048]{1,0:T(8,128)} fusion(f32[2048,512]{0,1:T(8,128)} %all-gather.12.cloned.1.call-done, f32[1024,128]{0,1:T(8,128)S(1)} %fusion.79, f32[1024,128]{0,1:T(8,128)S(1)} %fusion.13, f32[1024,128]{0,1:T(8,128)S(1)} %fusion.15, f32[1024,128]{0,1:T(8,128)S(1)} %fusion.17, f32[1024,2048]{1,0:T(8,128)} %param.7, ...), kind=kOutput, calls=%fused_computation.1 | convolution fusion | flops 6452412416 | bytes 27262976 | tf_op jit(solution)/shard_map/dot_general | solution.py:69
  (124 shorter events, 165.5 us)
Async XLA Ops:
  7.2 78.5 %all-gather.8.cloned.1.call-start = ((), (), s32[]{:S(2)}) async-start(), calls=%async_computation.2 | async-start | bytes 4718592 | tf_op jit(solution)/shard_map/all_gather | solution.py:49
  7.9 139.8 %all-reduce.5.cloned.1.call-start = ((), (), s32[]{:S(2)}) async-start(), calls=%async_computation.3 | async-start | bytes 4194304 | tf_op jit(solution)/shard_map/psum | solution.py:53
  97.7 181.5 %all-gather.14.cloned.1.call-start = ((), (), s32[]{:S(2)}) async-start(), calls=%async_computation.9 | async-start | bytes 9437184 | tf_op jit(solution)/shard_map/all_gather | solution.py:54
  154.5 331.5 %reduce-scatter.3.cloned.1.call-start = ((), (), s32[]{:S(2)}) async-start(), calls=%async_computation.4 | async-start | bytes 4718592 | tf_op jit(solution)/shard_map/reduce_scatter | solution.py:59
  283.7 98.1 %copy-start.2 = (f32[1024,512]{1,0:T(8,128)S(1)}, f32[1024,512]{1,0:T(8,128)}, u32[]{:S(2)}) copy-start(f32[1024,512]{1,0:T(8,128)} %all-reduce.5.cloned.1.call-done) | copy-start | bytes 6291460
  307.9 0.8 copy-start.5
  384.3 3.9 copy-start
  399.3 86.8 %copy-start.8 = (u32[32]{0:T(128)S(1)}, u32[32]{0:T(128)}, u32[]{:S(2)}) copy-start(u32[32]{0:T(128)} %constant.27) | copy-start | bytes 388
  399.3 161.4 %all-gather.10.cloned.1.call-start = ((), (), s32[]{:S(2)}) async-start(), calls=%async_computation.5 | async-start | bytes 4718592 | tf_op jit(solution)/shard_map/all_gather | solution.py:64
  486.0 137.0 %all-reduce.7.cloned.1.call-start = ((), (), s32[]{:S(2)}) async-start(), calls=%async_computation.6 | async-start | bytes 4194304 | tf_op jit(solution)/shard_map/psum | solution.py:53
  572.9 181.5 %all-gather.16.cloned.1.call-start = ((), (), s32[]{:S(2)}) async-start(), calls=%async_computation.10 | async-start | bytes 9437184 | tf_op jit(solution)/shard_map/all_gather | solution.py:54
  629.8 331.1 %reduce-scatter.5.cloned.1.call-start = ((), (), s32[]{:S(2)}) async-start(), calls=%async_computation.7 | async-start | bytes 4718592 | tf_op jit(solution)/shard_map/reduce_scatter | solution.py:59
  759.0 97.9 %copy-start.3 = (f32[1024,512]{1,0:T(8,128)S(1)}, f32[1024,512]{1,0:T(8,128)}, u32[]{:S(2)}) copy-start(f32[1024,512]{1,0:T(8,128)} %all-reduce.7.cloned.1.call-done) | copy-start | bytes 6291460
  783.1 0.8 copy-start.6
  859.4 3.9 copy-start.1
  874.2 161.5 %all-gather.12.cloned.1.call-start = ((), (), s32[]{:S(2)}) async-start(), calls=%async_computation.8 | async-start | bytes 4718592 | tf_op jit(solution)/shard_map/all_gather | solution.py:64
  1035.8 13.9 %copy-start.4 = (f32[2048,512]{0,1:T(8,128)S(1)}, f32[2048,512]{0,1:T(8,128)}, u32[]{:S(2)}) copy-start(f32[2048,512]{0,1:T(8,128)} %all-gather.12.cloned.1.call-done) | copy-start | bytes 12582916
  1035.8 13.9 %copy-start.7 = (bf16[1024,2048]{1,0:T(8,128)(2,1)S(1)}, bf16[1024,2048]{1,0:T(8,128)(2,1)}, u32[]{:S(2)}) copy-start(bf16[1024,2048]{1,0:T(8,128)(2,1)} %param.9) | copy-start | bytes 12582916
Sparse Core Ops, SparseCore 0:
  10.1 75.5 all-gather.7
  97.8 49.9 all-reduce.4
  154.6 124.5 all-gather.13
  399.5 86.4 reduce-scatter.2
  488.0 72.7 all-gather.9
  573.1 49.8 all-reduce.6
  629.9 124.5 all-gather.15
  874.4 86.4 reduce-scatter.4
  963.0 72.7 all-gather.11
